TPU v7x, 256 devices: a whole 4x4x8 slice. The times are simulated.
256 devices in a mesh: space: 32 (over x, y, core), tm: 8 (over z).
Axes of the slice: x: 4, y: 4, z: 8, core: 2. Of those that a mesh axis runs over, the one named last changes fastest.
Arguments:
- velocity: bfloat16 [256, 2, 512, 1024], P('tm', None, 'space'), may hold values from -8.4 to 8.4
Outputs:
- vorticity: bfloat16 [256, 512, 1024], P('tm', 'space')
- modes: float32 [32, 512, 1024], P('tm', 'space')
All inputs are finite; a program needn't handle non-finite values.
Results may differ from a plain program's by a relative error of at most 0.003.
Values may be sent and summed in bfloat16 or wider, within the bound.
A program may use at most 64 MiB of HBM per device.

v0:
```python
import jax
import jax.numpy as jnp
from jax import lax
from jax.sharding import PartitionSpec as P

RANK = 32
HIGH = lax.Precision.HIGHEST


def halo_rows(block, width):
    count = lax.axis_size("space")
    forward = [(i, (i + 1) % count) for i in range(count)]
    backward = [(target, source) for source, target in forward]
    rows = block.shape[1]
    low = lax.ppermute(block[:, rows - width :], "space", forward)
    high = lax.ppermute(block[:, :width], "space", backward)
    return jnp.concatenate([low, block, high], axis=1)


def spanwise(field):
    ahead = jnp.roll(field, -1, 2)
    behind = jnp.roll(field, 1, 2)
    ahead_two = jnp.roll(field, -2, 2)
    behind_two = jnp.roll(field, 2, 2)
    return (8.0 * (ahead - behind) - (ahead_two - behind_two)) / 12.0


def merge_small(gram):
    coeffs = gram[:, :, :RANK] + gram[:, :, RANK:]
    diagonal = jnp.diagonal(gram, axis1=1, axis2=2)
    scales = jnp.sqrt(diagonal[:, :RANK] + diagonal[:, RANK:])
    half = jnp.einsum("nab,nbc->nac", gram, coeffs, precision=HIGH)
    inner = jnp.einsum("nab,nac->nbc", coeffs, half, precision=HIGH)
    lower = jnp.linalg.cholesky(inner)
    eye = jnp.broadcast_to(jnp.eye(RANK, dtype=jnp.float32), inner.shape)
    lower_inv = lax.linalg.triangular_solve(lower, eye, left_side=True, lower=True)
    factor = jnp.swapaxes(lower_inv, 1, 2) * scales[:, None, :]
    return jnp.einsum("nab,nbc->nac", coeffs, factor, precision=HIGH)


def tree_basis(gram, leaves):
    width = leaves * RANK
    basis = None
    span = 1
    while span < leaves:
        nodes = leaves // (2 * span)
        size = 2 * span * RANK
        sub = jnp.stack(
            [gram[k * size : (k + 1) * size, k * size : (k + 1) * size] for k in range(nodes)]
        )
        if basis is None:
            h = sub
        else:
            b = basis.reshape(nodes, 2, span * RANK, RANK)
            zero = jnp.zeros_like(b[:, 0])
            bd = jnp.concatenate(
                [
                    jnp.concatenate([b[:, 0], zero], axis=2),
                    jnp.concatenate([zero, b[:, 1]], axis=2),
                ],
                axis=1,
            )
            gb = jnp.einsum("nab,nbc->nac", sub, bd, precision=HIGH)
            h = jnp.einsum("nab,nac->nbc", bd, gb, precision=HIGH)
        c = merge_small(h)
        if basis is None:
            basis = c
        else:
            basis = jnp.einsum("nab,nbc->nac", bd, c, precision=HIGH)
        span *= 2
    return basis.reshape(width, RANK)


def local(velocity):
    rows = velocity.shape[2]
    span_v = halo_rows(velocity[:, 1], 2).astype(jnp.float32)
    stream_u = velocity[:, 0].astype(jnp.float32)
    dv_dx = (
        8.0 * (span_v[:, 3 : rows + 3] - span_v[:, 1 : rows + 1])
        - (span_v[:, 4:] - span_v[:, :rows])
    ) / 12.0
    vorticity = (dv_dx - spanwise(stream_u)).astype(jnp.bfloat16)
    blocks = lax.axis_size("tm")
    cells = lax.all_to_all(vorticity, "tm", 2, 0, tiled=True)
    flat = cells.reshape(cells.shape[0], -1)
    gram = jnp.einsum("ax,bx->ab", flat, flat, preferred_element_type=jnp.float32)
    gram = lax.psum(gram, ("space", "tm"))
    basis = tree_basis(gram, blocks)
    part = jnp.einsum("ab,ax->bx", basis, flat.astype(jnp.float32), precision=HIGH).reshape(
        RANK, rows, -1
    )
    modes = lax.all_to_all(part, "tm", 0, 2, tiled=True)
    return (vorticity, modes)


def solution(mesh):
    in_specs = (P("tm", None, "space", None),)
    out_specs = (P("tm", "space", None), P("tm", "space", None))
    return jax.shard_map(local, mesh=mesh, in_specs=in_specs, out_specs=out_specs, check_vma=False)
```

profile of v0, /device:TPU:2, one launch (start us, length us, event | category | flops | bytes accessed | tf_op | source)
XLA Modules:
  0.0 411.2 jit_solution(9131504356403751906)
XLA Ops:
  7.2 1.9 bitcast_convert_fusion
  9.7 3.8 collective-permute-start.1
  15.4 0.8 collective-permute-done
  17.2 2.2 fusion.3
  19.4 5.1 %copy.130 = bf16[32,16,1024]{0,1,2:T(8,128)(2,1)} copy(bf16[32,16,1024]{2,1,0:T(8,128)(2,1)S(1)} %fusion.3) | data formatting | bytes 2097152 | tf_op jit(solution)/shard_map/convert_element_type | solution.py:82
  24.5 7.8 %reshape.157 = bf16[8,2,32768]{2,1,0:T(2,128)(2,1)} reshape(bf16[1024,16,32]{2,1,0:T(8,128)(2,1)} %bitcast.133) | data formatting | bytes 2097152
  32.4 8.5 %all-to-all-start = ((bf16[8,2,32768]{2,1,0:T(2,128)(2,1)}), bf16[8,2,32768]{2,1,0:T(2,128)(2,1)S(1)}, u32[]{:S(2)}, u32[]{:S(2)}) async-start(bf16[8,2,32768]{2,1,0:T(2,128)(2,1)} %reshape.157), calls=%async_computation | async-start | bytes 2097152 | tf_op jit(solution)/shard_map/all_to_all | solution.py:84
  41.1 28.5 %all-to-all-done = bf16[8,2,32768]{2,1,0:T(2,128)(2,1)S(1)} async-done(((bf16[8,2,32768]{2,1,0:T(2,128)(2,1)}), bf16[8,2,32768]{2,1,0:T(2,128)(2,1)S(1)}, u32[]{:S(2)}, u32[]{:S(2)}) %all-to-all-start) | async-done | bytes 1048608 | tf_op jit(solution)/shard_map/all_to_all | solution.py:84
  69.6 4.5 %reshape.158 = bf16[1024,16,32]{2,1,0:T(8,128)(2,1)} reshape(bf16[8,2,32768]{2,1,0:T(2,128)(2,1)S(1)} %all-to-all-done) | data formatting | bytes 2097152
  74.1 5.4 %copy.131 = bf16[32,16,8,128]{3,1,0,2:T(8,128)(2,1)S(1)} copy(bf16[32,16,8,128]{0,1,3,2:T(8,128)(2,1)} %bitcast.132) | data formatting | bytes 2097152 | tf_op jit(solution)/shard_map/all_to_all | solution.py:84
  79.5 1.2 fusion.10
  82.2 244.6 %all-reduce.6.cloned.1.call-done = f32[256,256]{0,1:T(8,128)} async-done(((f32[256,256]{0,1:T(8,128)}), f32[256,256]{0,1:T(8,128)}) %all-reduce.6.cloned.1.call-update) | async-done | bytes 262160 | tf_op jit(solution)/shard_map/psum | solution.py:87
  326.8 0.9 slice_bitcast_fusion.7
  327.8 1.9 copy.137
  329.7 0.9 fusion.70
  330.6 1.5 gather_fusion
  332.0 0.8 copy.138
  332.9 1.1 fusion.69
  334.1 11.7 %custom-call.21 = f32[4,32,32]{2,1,0:T(8,128)S(1)} custom-call(f32[4,32,32]{2,1,0:T(8,128)S(1)} %fusion.19), custom_call_target="Cholesky" | custom-call | tf_op jit(solution)/shard_map/jit(cholesky)/cholesky | solution.py:34
  346.1 9.8 %custom-call.22 = f32[4,1,32,32]{2,3,1,0:T(8,128)S(1)} custom-call(f32[4,1,32,32]{3,2,1,0:T(8,128)S(1)} %select_bitcast_fusion), custom_call_target="InvertDiagBlocksLowerTriangular" | custom-call | tf_op jit(solution)/shard_map/triangular_solve | solution.py:36
  355.9 0.9 convolution_multiply_fusion
  357.8 1.9 copy.147
  360.5 1.5 gather_fusion.1
  362.0 0.8 copy.148
  362.9 0.9 fusion.66
  363.9 5.9 %custom-call.23 = f32[2,32,32]{2,1,0:T(8,128)S(1)} custom-call(f32[2,32,32]{2,1,0:T(8,128)S(1)} %fusion.32), custom_call_target="Cholesky" | custom-call | tf_op jit(solution)/shard_map/jit(cholesky)/cholesky | solution.py:34
  370.0 4.9 %custom-call.24 = f32[2,1,32,32]{2,3,1,0:T(8,128)S(1)} custom-call(f32[2,1,32,32]{3,2,1,0:T(8,128)S(1)} %select_bitcast_fusion.1), custom_call_target="InvertDiagBlocksLowerTriangular" | custom-call | tf_op jit(solution)/shard_map/triangular_solve | solution.py:36
  375.0 0.9 convolution_multiply_fusion.1
  378.1 2.9 custom-call.25
  382.3 2.4 custom-call.26
  385.4 1.0 fusion.76
  386.6 17.1 %all_to_all.33 = f32[32,16,128]{2,1,0:T(8,128)S(1)} all-to-all(f32[32,16,128]{2,1,0:T(8,128)S(1)} %copy.153), channel_id=1, replica_groups=mesh['space'=32,'tm'=8] {'tm'}, dimensions={0} | all-to-all | bytes 524288 | tf_op jit(solution)/shard_map/all_to_all | solution.py:92
  (61 shorter events, 12.6 us)
Async XLA Ops:
  9.6 6.6 %collective-permute-start = (bf16[32,2,1024]{2,0,1:T(8,128)(2,1)S(1)}, bf16[32,2,1024]{2,0,1:T(8,128)(2,1)S(1)}, u32[]{:S(2)}, u32[]{:S(2)}) collective-permute-start(bf16[32,2,1024]{2,0,1:T(8,128)(2,1)S(1)} %get-tuple-element.18), channel_id=1, source_target_pairs={{0,8},{8,16},{16,24},{24,32},{32,40},{40,48},{48,56},{56,64},{64,7... | collective-permute-start | bytes 393224 | tf_op jit(solution)/shard_map/ppermute | solution.py:15
  9.7 6.5 %collective-permute-start.1 = (bf16[32,2,1024]{2,0,1:T(8,128)(2,1)S(1)}, bf16[32,2,1024]{2,0,1:T(8,128)(2,1)S(1)}, u32[]{:S(2)}, u32[]{:S(2)}) collective-permute-start(bf16[32,2,1024]{2,0,1:T(8,128)(2,1)S(1)} %get-tuple-element.19), channel_id=1, source_target_pairs={{8,0},{16,8},{24,16},{32,24},{40,32},{48,40},{56,48},{64,56},{72,6... | collective-permute-start | bytes 393224 | tf_op jit(solution)/shard_map/ppermute | solution.py:16
  19.4 5.1 %copy-start = (bf16[32,16,1024]{2,1,0:T(8,128)(2,1)}, bf16[32,16,1024]{2,1,0:T(8,128)(2,1)S(1)}, u32[]{:S(2)}) copy-start(bf16[32,16,1024]{2,1,0:T(8,128)(2,1)S(1)} %fusion.3) | copy-start | bytes 3145732
  32.4 37.2 %all-to-all-start = ((bf16[8,2,32768]{2,1,0:T(2,128)(2,1)}), bf16[8,2,32768]{2,1,0:T(2,128)(2,1)S(1)}, u32[]{:S(2)}, u32[]{:S(2)}) async-start(bf16[8,2,32768]{2,1,0:T(2,128)(2,1)} %reshape.157), calls=%async_computation | async-start | bytes 2097152 | tf_op jit(solution)/shard_map/all_to_all | solution.py:84
  40.8 286.0 %all-reduce.6.cloned.1.call-start = ((), (), s32[]{:S(2)}) async-start(), calls=%async_computation.2 | async-start | bytes 524288 | tf_op jit(solution)/shard_map/psum | solution.py:87
  327.7 29.5 %copy-start.1 = (f32[256,256]{0,1:T(8,128)S(1)}, f32[256,256]{0,1:T(8,128)}, u32[]{:S(2)}) copy-start(f32[256,256]{0,1:T(8,128)} %all-reduce.6.cloned.1.call-done) | copy-start | bytes 786436
Sparse Core Ops, SparseCore 0:
  80.8 245.9 all-reduce.5
where the time goes:
time: 412 us; the launch traced here: 411 us
  waiting for transfers between devices  274 us (67%)
  other arithmetic  44.8 us (11%)
  local copies, waits for them, and re-layouts  37.9 us (9%)
  blocking collectives  17.1 us (4%)
  between operations  14.4 us (3%)
  starting transfers between devices  12.6 us (3%)
  matrix products  10.4 us (3%)
    psum x1, waiting for transfers between devices, local(): gram = lax.psum(gram, ('space', 'tm'))  245 us
    all_to_all x1, waiting for transfers between devices, local(): cells = lax.all_to_all(vorticity, 'tm', 2, 0, tiled=True)  28.5 us
    another operation x9, other arithmetic, merge_small(): lower = jnp.linalg.cholesky(inner)  21.5 us
    another operation x7, other arithmetic, merge_small(): lax.linalg.triangular_solve(lower, eye, left_side=True, lower=True)  18 us
    all_to_all x1, blocking collectives, local(): modes = lax.all_to_all(part, 'tm', 0, 2, tiled=True)  17.1 us
    unnamed x8, local copies, waits for them, and re-layouts  13.2 us
    all_to_all x1, starting transfers between devices, local(): cells = lax.all_to_all(vorticity, 'tm', 2, 0, tiled=True)  8.47 us
  transfers between devices with their start and end apart: 4, of which 3 were waited for; matrix products, arithmetic and copies ran while one was open for 1% of the time, Pallas kernels for 0%

commit v1 on v0

--- a/solution.py
+++ b/solution.py
@@ -2,9 +2,41 @@
 import jax.numpy as jnp
 from jax import lax
 from jax.sharding import PartitionSpec as P
+from jax.lax import axis_index, axis_size, ppermute
 
 RANK = 32
 HIGH = lax.Precision.HIGHEST
+
+
+def lay_sample(piece_in, in_dim, work_x):
+    wide_out, v1 = (piece_in.shape[:in_dim], piece_in.shape[in_dim + 1 :])
+    w2 = piece_in.reshape(*wide_out, work_x, -1, *v1)
+    return jnp.moveaxis(w2, in_dim, 0)
+
+
+def obtain_meshes(load, array_axis):
+    carry = list(load.shape[1:])
+    carry[array_axis] *= load.shape[0]
+    return jnp.moveaxis(load, 0, array_axis).reshape(carry)
+
+
+def mix_slabs_for(shard_in, lane_axis, original, slab_in):
+    y = axis_size(lane_axis)
+    before = axis_index(lane_axis)
+    block_last, t_next = (y, before)
+    z_new = lay_sample(shard_in, original, block_last)
+    chunks = [z_new[t_next]]
+    s = 1
+    while s < block_last:
+        all_values = z_new[t_next ^ s]
+        u_next = ppermute(
+            all_values, axis_name=lane_axis, perm=[(j, j ^ s) for j in range(block_last)]
+        )
+        chunks.append(u_next)
+        s += 1
+    upper = jnp.stack(chunks, 0)
+    z_new = upper[t_next ^ jnp.arange(block_last)]
+    return obtain_meshes(z_new, slab_in)
 
 
 def halo_rows(block, width):
@@ -81,7 +113,7 @@
     ) / 12.0
     vorticity = (dv_dx - spanwise(stream_u)).astype(jnp.bfloat16)
     blocks = lax.axis_size("tm")
-    cells = lax.all_to_all(vorticity, "tm", 2, 0, tiled=True)
+    cells = mix_slabs_for(vorticity, "tm", 2, 0)
     flat = cells.reshape(cells.shape[0], -1)
     gram = jnp.einsum("ax,bx->ab", flat, flat, preferred_element_type=jnp.float32)
     gram = lax.psum(gram, ("space", "tm"))

time: 412 us -> 400 us (0.971)
  waiting for transfers between devices: 274 us -> 259 us
  local copies, waits for them, and re-layouts: 37.9 us -> 24.5 us
  starting transfers between devices: 12.6 us -> 25.3 us
    all_to_all x1 -> x0, waiting for transfers between devices: 28.5 us -> none  [local(): cells = lax.all_to_all(vorticity, 'tm', 2, 0, tiled=True)]
    ppermute x0 -> x7, starting transfers between devices: none -> 21.4 us  [mix_slabs_for(): ppermute(all_values, axis_name=lane_axis, perm=[(j, j ^ s) for j in range...]
    ppermute x0 -> x7, waiting for transfers between devices: none -> 12.3 us  [mix_slabs_for(): ppermute(all_values, axis_name=lane_axis, perm=[(j, j ^ s) for j in range...]
    unnamed x8 -> x28, local copies, waits for them, and re-layouts: 13.2 us -> 1.37 us
    all_to_all x1 -> x0, starting transfers between devices: 8.47 us -> none  [local(): cells = lax.all_to_all(vorticity, 'tm', 2, 0, tiled=True)]
    all_to_all x1 -> x0, local copies, waits for them, and re-layouts: 5.35 us -> none  [local(): cells = lax.all_to_all(vorticity, 'tm', 2, 0, tiled=True)]
    convert_element_type x1 -> x0, local copies, waits for them, and re-layouts: 5.11 us -> none  [local(): vorticity = (dv_dx - spanwise(stream_u)).astype(jnp.bfloat16)]
  transfers between devices with their start and end apart: 4 -> 10, of which waited for: 3 -> 4; matrix products, arithmetic and copies ran while one was open for 1% -> 2% of each run, Pallas kernels for 0% -> 0%
where the time goes in v1:
time: 400 us; the launch traced here: 399 us
  waiting for transfers between devices  259 us (65%)
  other arithmetic  47.9 us (12%)
  starting transfers between devices  25.3 us (6%)
  local copies, waits for them, and re-layouts  24.5 us (6%)
  blocking collectives  17.1 us (4%)
  between operations  14.5 us (4%)
  matrix products  10.4 us (3%)
    psum x1, waiting for transfers between devices, local(): gram = lax.psum(gram, ('space', 'tm'))  247 us
    another operation x9, other arithmetic, merge_small(): lower = jnp.linalg.cholesky(inner)  21.5 us
    ppermute x7, starting transfers between devices, mix_slabs_for(): ppermute(all_values, axis_name=lane_axis, perm=[(j, j ^ s) for j in range...  21.4 us
    another operation x7, other arithmetic, merge_small(): lax.linalg.triangular_solve(lower, eye, left_side=True, lower=True)  18 us
    all_to_all x1, blocking collectives, local(): modes = lax.all_to_all(part, 'tm', 0, 2, tiled=True)  17.1 us
    ppermute x7, waiting for transfers between devices, mix_slabs_for(): ppermute(all_values, axis_name=lane_axis, perm=[(j, j ^ s) for j in range...  12.3 us
  transfers between devices with their start and end apart: 10, of which 4 were waited for; matrix products, arithmetic and copies ran while one was open for 2% of the time, Pallas kernels for 0%

profile of v1, /device:TPU:2, one launch (start us, length us, event | category | flops | bytes accessed | tf_op | source)
XLA Modules:
  0.0 399.0 jit_solution(8789973421365868783)
XLA Ops:
  7.2 1.9 bitcast_convert_fusion
  10.0 3.9 collective-permute-start.1
  13.9 2.2 fusion.73
  16.0 2.7 fusion.75
  21.6 1.7 maximum_convert_fusion
  23.9 3.3 fusion.3
  27.5 2.4 constant_dynamic-slice_fusion
  29.9 2.0 collective-permute-start.2
  31.9 3.4 collective-permute-start.3
  35.4 6.5 %collective-permute-start.5 = (bf16[32,16,128]{2,1,0:T(8,128)(2,1)S(1)}, bf16[32,16,128]{2,1,0:T(8,128)(2,1)S(1)}, u32[]{:S(2)}, u32[]{:S(2)}) collective-permute-start(bf16[32,16,128]{2,1,0:T(8,128)(2,1)S(1)} %bitcast.188), channel_id=1, source_target_pairs={{0,4},{1,5},{2,6},{3,7},{4,0},{5,1},{6,2},{7,3},{8,12},{9,13},{10,... | collective-permute-start | bytes 393224 | tf_op jit(solution)/shard_map/ppermute | solution.py:32
  42.1 4.7 %collective-permute-start.7 = (bf16[32,16,128]{2,1,0:T(8,128)(2,1)S(1)}, bf16[32,16,128]{2,1,0:T(8,128)(2,1)S(1)}, u32[]{:S(2)}, u32[]{:S(2)}) collective-permute-start(bf16[32,16,128]{2,1,0:T(8,128)(2,1)S(1)} %bitcast.186), channel_id=1, source_target_pairs={{0,6},{1,7},{2,4},{3,5},{4,2},{5,3},{6,0},{7,1},{8,14},{9,15},{10,... | collective-permute-start | bytes 393224 | tf_op jit(solution)/shard_map/ppermute | solution.py:32
  46.8 4.1 %collective-permute-done.3 = bf16[32,16,128]{2,1,0:T(8,128)(2,1)S(1)} collective-permute-done((bf16[32,16,128]{2,1,0:T(8,128)(2,1)S(1)}, bf16[32,16,128]{2,1,0:T(8,128)(2,1)S(1)}, u32[]{:S(2)}, u32[]{:S(2)}) %collective-permute-start.3) | collective-permute-done | bytes 131104 | tf_op jit(solution)/shard_map/ppermute | solution.py:32
  50.9 4.8 %collective-permute-start.8 = (bf16[32,16,128]{2,1,0:T(8,128)(2,1)S(1)}, bf16[32,16,128]{2,1,0:T(8,128)(2,1)S(1)}, u32[]{:S(2)}, u32[]{:S(2)}) collective-permute-start(bf16[32,16,128]{2,1,0:T(8,128)(2,1)S(1)} %bitcast.185), channel_id=1, source_target_pairs={{0,7},{1,6},{2,5},{3,4},{4,3},{5,2},{6,1},{7,0},{8,15},{9,14},{10,... | collective-permute-start | bytes 393224 | tf_op jit(solution)/shard_map/ppermute | solution.py:32
  55.7 4.2 %collective-permute-done.6 = bf16[32,16,128]{2,1,0:T(8,128)(2,1)S(1)} collective-permute-done((bf16[32,16,128]{2,1,0:T(8,128)(2,1)S(1)}, bf16[32,16,128]{2,1,0:T(8,128)(2,1)S(1)}, u32[]{:S(2)}, u32[]{:S(2)}) %collective-permute-start.6) | collective-permute-done | bytes 131104 | tf_op jit(solution)/shard_map/ppermute | solution.py:32
  60.0 4.0 collective-permute-done.8
  64.9 1.2 fusion.10
  67.6 247.0 %all-reduce.6.cloned.1.call-done = f32[256,256]{0,1:T(8,128)} async-done(((f32[256,256]{0,1:T(8,128)}), f32[256,256]{0,1:T(8,128)}) %all-reduce.6.cloned.1.call-update) | async-done | bytes 262160 | tf_op jit(solution)/shard_map/psum | solution.py:119
  315.5 1.9 copy.115
  318.3 1.5 gather_fusion.1
  320.7 1.1 fusion.70
  321.9 11.7 %custom-call.21 = f32[4,32,32]{2,1,0:T(8,128)S(1)} custom-call(f32[4,32,32]{2,1,0:T(8,128)S(1)} %fusion.19), custom_call_target="Cholesky" | custom-call | tf_op jit(solution)/shard_map/jit(cholesky)/cholesky | solution.py:66
  333.9 9.8 %custom-call.22 = f32[4,1,32,32]{2,3,1,0:T(8,128)S(1)} custom-call(f32[4,1,32,32]{3,2,1,0:T(8,128)S(1)} %select_bitcast_fusion), custom_call_target="InvertDiagBlocksLowerTriangular" | custom-call | tf_op jit(solution)/shard_map/triangular_solve | solution.py:68
  343.7 0.9 convolution_multiply_fusion
  345.6 1.9 copy.125
  348.3 1.5 gather_fusion.2
  350.7 0.9 fusion.67
  351.7 5.9 %custom-call.23 = f32[2,32,32]{2,1,0:T(8,128)S(1)} custom-call(f32[2,32,32]{2,1,0:T(8,128)S(1)} %fusion.32), custom_call_target="Cholesky" | custom-call | tf_op jit(solution)/shard_map/jit(cholesky)/cholesky | solution.py:66
  357.8 4.9 %custom-call.24 = f32[2,1,32,32]{2,3,1,0:T(8,128)S(1)} custom-call(f32[2,1,32,32]{3,2,1,0:T(8,128)S(1)} %select_bitcast_fusion.1), custom_call_target="InvertDiagBlocksLowerTriangular" | custom-call | tf_op jit(solution)/shard_map/triangular_solve | solution.py:68
  365.8 2.9 custom-call.25
  370.1 2.4 custom-call.26
  373.2 1.0 fusion.77
  374.3 17.1 %all_to_all.18 = f32[32,16,128]{2,1,0:T(8,128)S(1)} all-to-all(f32[32,16,128]{2,1,0:T(8,128)S(1)} %copy.131), channel_id=1, replica_groups=mesh['space'=32,'tm'=8] {'tm'}, dimensions={0} | all-to-all | bytes 524288 | tf_op jit(solution)/shard_map/all_to_all | solution.py:124
  (95 shorter events, 19.3 us)
Async XLA Ops:
  7.2 307.4 %all-reduce.6.cloned.1.call-start = ((), (), s32[]{:S(2)}) async-start(), calls=%async_computation.1 | async-start | bytes 524288 | tf_op jit(solution)/shard_map/psum | solution.py:119
  10.0 11.6 %collective-permute-start = (bf16[32,2,1024]{2,1,0:T(2,128)(2,1)}, bf16[32,2,1024]{2,1,0:T(2,128)(2,1)S(1)}, u32[]{:S(2)}, u32[]{:S(2)}) collective-permute-start(bf16[32,2,1024]{2,1,0:T(2,128)(2,1)} %get-tuple-element.20), channel_id=1, source_target_pairs={{0,8},{8,16},{16,24},{24,32},{32,40},{40,48},{48,56},{56,64},{64,7... | collective-permute-start | bytes 393224 | tf_op jit(solution)/shard_map/ppermute | solution.py:47
  10.0 11.6 %collective-permute-start.1 = (bf16[32,2,1024]{2,1,0:T(2,128)(2,1)}, bf16[32,2,1024]{2,1,0:T(2,128)(2,1)}, u32[]{:S(2)}, u32[]{:S(2)}) collective-permute-start(bf16[32,2,1024]{2,1,0:T(2,128)(2,1)} %get-tuple-element.21), channel_id=1, source_target_pairs={{8,0},{16,8},{24,16},{32,24},{40,32},{48,40},{56,48},{64,56},{72,6... | collective-permute-start | bytes 393224 | tf_op jit(solution)/shard_map/ppermute | solution.py:48
  21.6 1.7 copy-start
  21.6 2.3 copy-start.1
  21.6 2.3 copy-start.3
  27.2 2.7 copy-start.2
  29.9 12.2 %collective-permute-start.2 = (bf16[32,16,128]{2,1,0:T(8,128)(2,1)S(1)}, bf16[32,16,128]{2,1,0:T(8,128)(2,1)S(1)}, u32[]{:S(2)}, u32[]{:S(2)}) collective-permute-start(bf16[32,16,128]{2,1,0:T(8,128)(2,1)S(1)} %bitcast.191), channel_id=1, source_target_pairs={{0,1},{1,0},{2,3},{3,2},{4,5},{5,4},{6,7},{7,6},{8,9},{9,8},{10,11... | collective-permute-start | bytes 393224 | tf_op jit(solution)/shard_map/ppermute | solution.py:32
  31.9 18.9 %collective-permute-start.3 = (bf16[32,16,128]{2,1,0:T(8,128)(2,1)S(1)}, bf16[32,16,128]{2,1,0:T(8,128)(2,1)S(1)}, u32[]{:S(2)}, u32[]{:S(2)}) collective-permute-start(bf16[32,16,128]{2,1,0:T(8,128)(2,1)S(1)} %bitcast.190), channel_id=1, source_target_pairs={{0,2},{1,3},{2,0},{3,1},{4,6},{5,7},{6,4},{7,5},{8,10},{9,11},{10,... | collective-permute-start | bytes 393224 | tf_op jit(solution)/shard_map/ppermute | solution.py:32
  35.3 20.4 %collective-permute-start.4 = (bf16[32,16,128]{2,1,0:T(8,128)(2,1)S(1)}, bf16[32,16,128]{2,1,0:T(8,128)(2,1)S(1)}, u32[]{:S(2)}, u32[]{:S(2)}) collective-permute-start(bf16[32,16,128]{2,1,0:T(8,128)(2,1)S(1)} %bitcast.189), channel_id=1, source_target_pairs={{0,3},{1,2},{2,1},{3,0},{4,7},{5,6},{6,5},{7,4},{8,11},{9,10},{10,... | collective-permute-start | bytes 393224 | tf_op jit(solution)/shard_map/ppermute | solution.py:32
  35.4 20.3 %collective-permute-start.5 = (bf16[32,16,128]{2,1,0:T(8,128)(2,1)S(1)}, bf16[32,16,128]{2,1,0:T(8,128)(2,1)S(1)}, u32[]{:S(2)}, u32[]{:S(2)}) collective-permute-start(bf16[32,16,128]{2,1,0:T(8,128)(2,1)S(1)} %bitcast.188), channel_id=1, source_target_pairs={{0,4},{1,5},{2,6},{3,7},{4,0},{5,1},{6,2},{7,3},{8,12},{9,13},{10,... | collective-permute-start | bytes 393224 | tf_op jit(solution)/shard_map/ppermute | solution.py:32
  41.9 18.0 %collective-permute-start.6 = (bf16[32,16,128]{2,1,0:T(8,128)(2,1)S(1)}, bf16[32,16,128]{2,1,0:T(8,128)(2,1)S(1)}, u32[]{:S(2)}, u32[]{:S(2)}) collective-permute-start(bf16[32,16,128]{2,1,0:T(8,128)(2,1)S(1)} %bitcast.187), channel_id=1, source_target_pairs={{0,5},{1,4},{2,7},{3,6},{4,1},{5,0},{6,3},{7,2},{8,13},{9,12},{10,... | collective-permute-start | bytes 393224 | tf_op jit(solution)/shard_map/ppermute | solution.py:32
  42.1 17.9 %collective-permute-start.7 = (bf16[32,16,128]{2,1,0:T(8,128)(2,1)S(1)}, bf16[32,16,128]{2,1,0:T(8,128)(2,1)S(1)}, u32[]{:S(2)}, u32[]{:S(2)}) collective-permute-start(bf16[32,16,128]{2,1,0:T(8,128)(2,1)S(1)} %bitcast.186), channel_id=1, source_target_pairs={{0,6},{1,7},{2,4},{3,5},{4,2},{5,3},{6,0},{7,1},{8,14},{9,15},{10,... | collective-permute-start | bytes 393224 | tf_op jit(solution)/shard_map/ppermute | solution.py:32
  50.9 13.1 %collective-permute-start.8 = (bf16[32,16,128]{2,1,0:T(8,128)(2,1)S(1)}, bf16[32,16,128]{2,1,0:T(8,128)(2,1)S(1)}, u32[]{:S(2)}, u32[]{:S(2)}) collective-permute-start(bf16[32,16,128]{2,1,0:T(8,128)(2,1)S(1)} %bitcast.185), channel_id=1, source_target_pairs={{0,7},{1,6},{2,5},{3,4},{4,3},{5,2},{6,1},{7,0},{8,15},{9,14},{10,... | collective-permute-start | bytes 393224 | tf_op jit(solution)/shard_map/ppermute | solution.py:32
  67.6 266.0 %copy-start.5 = (pred[32,32]{1,0:T(8,128)(4,1)S(1)}, pred[32,32]{1,0:T(8,128)(4,1)}, u32[]{:S(2)}) copy-start(pred[32,32]{1,0:T(8,128)(4,1)} %iota_compare_fusion.7) | copy-start | bytes 3076
  315.5 29.5 %copy-start.4 = (f32[256,256]{0,1:T(8,128)S(1)}, f32[256,256]{0,1:T(8,128)}, u32[]{:S(2)}) copy-start(f32[256,256]{0,1:T(8,128)} %all-reduce.6.cloned.1.call-done) | copy-start | bytes 786436
Sparse Core Ops, SparseCore 0:
  66.2 248.3 all-reduce.5
